TPU v7x, 32 devices: a whole 2x2x4 slice. The times are simulated.
32 devices in a mesh: gx: 4 (over z), gy: 4 (over y, x), gz: 2 (over core).
Axes of the slice: x: 2, y: 2, z: 4, core: 2. Of those that a mesh axis runs over, the one named last changes fastest.
Arguments:
- velocity: float32 [3, 64, 64, 256], P(None, 'gx', 'gy', 'gz'), may hold values from -6 to 6
Outputs:
- stress_residual: float32 [6, 2048], P(None, ('gx', 'gy', 'gz'))
- coefficients: float32 [96, 6], replicated
All inputs are finite; a program needn't handle non-finite values.
Results may differ from a plain program's by a relative error of at most 0.0042.
Values may be sent and summed in bfloat16 or wider, within the bound.
No kernel may reach another device: no remote copies, remote signals or barrier semaphores. Data moves between devices by JAX's collectives and lax.ppermute only.
A program may use at most 64 MiB of HBM per device.

v0:
```python
import jax
import jax.numpy as jnp
import numpy as np
from jax import lax
from jax.sharding import PartitionSpec as P

PRECISE = lax.Precision.HIGHEST
INDEX_PAIRS = ((0, 0), (1, 1), (2, 2), (0, 1), (0, 2), (1, 2))
WIDTHS = (3.0, 6.0, 12.0)


def extended(block, sides, width):
    for axis, dim in sides:
        count = lax.axis_size(axis)
        forward = [(i, i + 1) for i in range(count - 1)]
        forward.append((count - 1, 0))
        backward = [(target, source) for source, target in forward]
        low = lax.ppermute(
            lax.slice_in_dim(block, block.shape[dim] - width, None, axis=dim), axis, forward
        )
        high = lax.ppermute(lax.slice_in_dim(block, 0, width, axis=dim), axis, backward)
        block = jnp.concatenate([low, block, high], axis=dim)
    return block


def window_table(combos):
    weights_table = np.zeros((len(combos), 16), np.float32)
    for row_index in range(len(combos)):
        box_width, offset = combos[row_index]
        low_edge = 7.5 + offset - box_width / 2.0
        high_edge = 7.5 + offset + box_width / 2.0
        for cell_index in range(16):
            cell_share = min(cell_index + 0.5, high_edge) - max(cell_index - 0.5, low_edge)
            weights_table[row_index, cell_index] = max(cell_share, 0.0) / box_width
    return weights_table


def velocity_combos():
    return [(box_width, offset) for box_width in WIDTHS for offset in (-2.0, 0.0, 2.0)]


def product_combos():
    return [(3.0, 0.0), (12.0, 0.0)]


def matrix_product(left_matrix, right_matrix):
    return [
        [
            left_matrix[i][0] * right_matrix[0][j]
            + left_matrix[i][1] * right_matrix[1][j]
            + left_matrix[i][2] * right_matrix[2][j]
            for j in range(3)
        ]
        for i in range(3)
    ]


def pick_pairs(matrix):
    return [matrix[i][j] for i, j in INDEX_PAIRS]


def build_rows(box_means, pair_means):
    feature_rows = []
    centre_values = []
    for width_index in range(3):
        middle = 3 * width_index + 1
        scaled = WIDTHS[width_index] ** 2 * 0.25

        def offset_value(component, direction, step_size):
            position_list = [middle, middle, middle]
            position_list[direction] = middle + step_size
            return box_means[component, position_list[0], position_list[1], position_list[2]]

        centre_values.append([box_means[i, middle, middle, middle] for i in range(3)])
        gradient = [
            [(offset_value(i, j, 1) - offset_value(i, j, -1)) * scaled for j in range(3)]
            for i in range(3)
        ]
        strain = [[(gradient[i][j] + gradient[j][i]) * 0.5 for j in range(3)] for i in range(3)]
        spin_part = [[(gradient[i][j] - gradient[j][i]) * 0.5 for j in range(3)] for i in range(3)]
        square_strain = matrix_product(strain, strain)
        first_order = matrix_product(strain, spin_part)
        second_order = matrix_product(spin_part, strain)
        commutator = [[first_order[i][j] - second_order[i][j] for j in range(3)] for i in range(3)]
        spin_square = matrix_product(spin_part, spin_part)
        magnitude = sum((strain[i][j] * strain[i][j] for i in range(3) for j in range(3)))
        feature_rows += (
            pick_pairs(strain)
            + pick_pairs(square_strain)
            + pick_pairs(commutator)
            + pick_pairs(spin_square)
        )
        feature_rows += [magnitude * entry for entry in pick_pairs(strain)]
    small_box = centre_values[0]
    large_box = centre_values[2]
    feature_rows += [
        pair_means[index, 0] - small_box[i] * small_box[j]
        for index, (i, j) in enumerate(INDEX_PAIRS)
    ]
    target_rows = [
        pair_means[index, 1] - large_box[i] * large_box[j]
        for index, (i, j) in enumerate(INDEX_PAIRS)
    ]
    return (jnp.stack(feature_rows), jnp.stack(target_rows))


def solve_fit(gram_matrix, sample_total):
    scales = jnp.sqrt(jnp.diagonal(gram_matrix) / sample_total + 1e-06)
    feature_scale = scales[:96]
    normal = gram_matrix[:96, :96] / (
        sample_total * feature_scale[:, None] * feature_scale[None, :]
    ) + 0.1 * jnp.eye(96, dtype=jnp.float32)
    target_side = gram_matrix[:96, 96:] / (sample_total * feature_scale[:, None])
    factor = jnp.linalg.cholesky(normal)
    solved = jax.scipy.linalg.cho_solve((factor, True), target_side)
    return (solved / feature_scale[:, None], scales[96:])


def axis_weights(length, weights_table):
    sample_count = length // 8
    combo_count = weights_table.shape[0]
    full_table = np.zeros((sample_count * combo_count, length + 8), np.float32)
    for sample_index in range(sample_count):
        full_table[
            sample_index * combo_count : (sample_index + 1) * combo_count,
            8 * sample_index : 8 * sample_index + 16,
        ] = weights_table
    return jnp.asarray(full_table)


def windowed(wide_field, weights_table):
    along_z = jnp.einsum(
        "cxyz,kz->cxyk",
        wide_field,
        axis_weights(wide_field.shape[3] - 8, weights_table),
        precision=PRECISE,
    )
    along_y = jnp.einsum(
        "cxyk,jy->cxjk",
        along_z,
        axis_weights(wide_field.shape[2] - 8, weights_table),
        precision=PRECISE,
    )
    return jnp.einsum(
        "cxjk,ix->cijk",
        along_y,
        axis_weights(wide_field.shape[1] - 8, weights_table),
        precision=PRECISE,
    )


def shards(velocity):
    rounded = velocity.astype(jnp.bfloat16)
    padded = extended(rounded, (("gx", 1), ("gy", 2), ("gz", 3)), 4)
    wide_field = padded.astype(jnp.float32)
    count_x = velocity.shape[1] // 8
    count_y = velocity.shape[2] // 8
    count_z = velocity.shape[3] // 8
    samples = count_x * count_y * count_z
    box_means = windowed(wide_field, window_table(velocity_combos()))
    box_means = box_means.reshape(3, count_x, 9, count_y, 9, count_z, 9)
    box_means = jnp.transpose(box_means, (0, 2, 4, 6, 1, 3, 5)).reshape(3, 9, 9, 9, samples)
    pair_field = jnp.stack([wide_field[i] * wide_field[j] for i, j in INDEX_PAIRS])
    pair_means = windowed(pair_field, window_table(product_combos())).reshape(
        6, count_x, 2, count_y, 2, count_z, 2
    )
    pair_means = jnp.stack(
        [pair_means[:, :, 0, :, 0, :, 0], pair_means[:, :, 1, :, 1, :, 1]], axis=1
    )
    pair_means = pair_means.reshape(6, 2, samples)
    features, targets = build_rows(box_means, pair_means)
    stacked = jnp.concatenate([features, targets], axis=0)
    local_gram = jnp.dot(stacked, stacked.T, precision=PRECISE, preferred_element_type=jnp.float32)
    gram_matrix = lax.psum(local_gram, ("gx", "gy", "gz"))
    sample_total = float(samples * lax.axis_size("gx") * lax.axis_size("gy") * lax.axis_size("gz"))
    coefficients, target_scale = solve_fit(gram_matrix, sample_total)
    predicted = jnp.dot(
        coefficients.T, features, precision=PRECISE, preferred_element_type=jnp.float32
    )
    residual = (targets - predicted) / target_scale[:, None]
    return (residual, coefficients)


def solution(mesh):
    in_specs = (P(None, "gx", "gy", "gz"),)
    out_specs = (P(None, ("gx", "gy", "gz")), P())
    return jax.shard_map(shards, mesh=mesh, in_specs=in_specs, out_specs=out_specs, check_vma=False)
```

profile of v0, /device:TPU:0, one launch (start us, length us, event | category | flops | bytes accessed | tf_op | source)
XLA Modules:
  0.0 118.4 jit_solution(10109509089073360371)
XLA Ops:
  0.6 1.0 convert_element_type.7
  1.7 0.0 copy-start.8
  1.7 3.1 %collective-permute-start = (bf16[3,4,16,128]{3,2,1,0:T(8,128)(2,1)S(1)}, bf16[3,4,16,128]{3,2,1,0:T(8,128)(2,1)S(1)}, u32[]{:S(2)}, u32[]{:S(2)}) collective-permute-start(bf16[3,4,16,128]{3,2,1,0:T(8,128)(2,1)S(1)} %get-tuple-element.102), channel_id=1, source_target_pairs={{0,8},{8,16},{16,24},{24,0},{1,9},{9,17},{17,25},{25,1},{2,10},{10... | collective-permute-start | bytes 147464 | tf_op jit(solution)/shard_map/ppermute | solution.py:18
  4.8 2.1 %collective-permute-start.1 = (bf16[3,4,16,128]{3,2,1,0:T(8,128)(2,1)S(1)}, bf16[3,4,16,128]{3,2,1,0:T(8,128)(2,1)S(1)}, u32[]{:S(2)}, u32[]{:S(2)}) collective-permute-start(bf16[3,4,16,128]{3,2,1,0:T(8,128)(2,1)S(1)} %get-tuple-element.103), channel_id=1, source_target_pairs={{8,0},{16,8},{24,16},{0,24},{9,1},{17,9},{25,17},{1,25},{10,2},{18... | collective-permute-start | bytes 147464 | tf_op jit(solution)/shard_map/ppermute | solution.py:21
  6.9 2.1 %collective-permute-done = bf16[3,4,16,128]{3,2,1,0:T(8,128)(2,1)S(1)} collective-permute-done((bf16[3,4,16,128]{3,2,1,0:T(8,128)(2,1)S(1)}, bf16[3,4,16,128]{3,2,1,0:T(8,128)(2,1)S(1)}, u32[]{:S(2)}, u32[]{:S(2)}) %collective-permute-start) | collective-permute-done | bytes 49184 | tf_op jit(solution)/shard_map/ppermute | solution.py:18
  9.0 0.4 collective-permute-done.1
  9.4 0.1 pad_maximum_fusion.4
  9.5 1.5 %collective-permute-start.2 = (bf16[3,24,4,128]{3,2,1,0:T(4,128)(2,1)S(1)}, bf16[3,24,4,128]{3,2,1,0:T(4,128)(2,1)S(1)}, u32[]{:S(2)}, u32[]{:S(2)}) collective-permute-start(bf16[3,24,4,128]{3,2,1,0:T(4,128)(2,1)S(1)} %get-tuple-element.100), channel_id=1, source_target_pairs={{0,2},{2,4},{4,6},{6,0},{1,3},{3,5},{5,7},{7,1},{8,10},{10,12},{12... | collective-permute-start | bytes 221192 | tf_op jit(solution)/shard_map/ppermute | solution.py:18
  11.0 1.4 %collective-permute-start.3 = (bf16[3,24,4,128]{3,2,1,0:T(4,128)(2,1)S(1)}, bf16[3,24,4,128]{3,2,1,0:T(4,128)(2,1)S(1)}, u32[]{:S(2)}, u32[]{:S(2)}) collective-permute-start(bf16[3,24,4,128]{3,2,1,0:T(4,128)(2,1)S(1)} %get-tuple-element.101), channel_id=1, source_target_pairs={{2,0},{4,2},{6,4},{0,6},{3,1},{5,3},{7,5},{1,7},{10,8},{12,10},{14... | collective-permute-start | bytes 221192 | tf_op jit(solution)/shard_map/ppermute | solution.py:21
  12.5 2.3 %collective-permute-done.2 = bf16[3,24,4,128]{3,2,1,0:T(4,128)(2,1)S(1)} collective-permute-done((bf16[3,24,4,128]{3,2,1,0:T(4,128)(2,1)S(1)}, bf16[3,24,4,128]{3,2,1,0:T(4,128)(2,1)S(1)}, u32[]{:S(2)}, u32[]{:S(2)}) %collective-permute-start.2) | collective-permute-done | bytes 73760 | tf_op jit(solution)/shard_map/ppermute | solution.py:18
  14.8 0.8 collective-permute-done.3
  15.6 0.2 pad_maximum_fusion.1
  15.9 0.2 fusion.156
  16.1 0.1 collective-permute-start.4
  16.2 0.5 collective-permute-start.5
  16.7 1.3 %collective-permute-done.4 = bf16[3,24,24,4]{3,2,1,0:T(8,128)(2,1)S(1)} collective-permute-done((bf16[3,24,24,4]{3,2,1,0:T(8,128)(2,1)S(1)}, bf16[3,24,24,4]{3,2,1,0:T(8,128)(2,1)S(1)}, u32[]{:S(2)}, u32[]{:S(2)}) %collective-permute-start.4) | collective-permute-done | bytes 13856 | tf_op jit(solution)/shard_map/ppermute | solution.py:18
  17.9 0.6 collective-permute-done.5
  18.6 0.0 copy-done.8
  18.6 1.3 %fusion.124 = f32[3,24,24,144]{3,2,1,0:T(8,128)S(1)} fusion(f32[144,136,1,1]{0,1,3,2:T(8,128)S(1)} %copy-done.8, bf16[3,24,24,4]{3,2,1,0:T(8,128)(2,1)S(1)} %collective-permute-done.5, bf16[3,24,4,128]{3,2,1,0:T(4,128)(2,1)S(1)} %collective-permute-done.3, bf16[3,4,16,128]{3,2,1,0:T(8,128)(2,1)S(1)} %collective-permute-done.1, ...), kind=kOutput, calls=%fused_computation.402 | convolution fusion | flops 409383936 | bytes 1543680 | tf_op jit(solution)/shard_map/cxyz,kz->cxyk/dot_general | solution.py:132
  19.9 1.6 %convolution_bitcast_fusion = f32[3,24,18,144]{3,2,1,0:T(8,128)S(1)} fusion(f32[3,24,24,144]{3,2,1,0:T(8,128)S(1)} %fusion.124, f32[18,24,1,1]{1,0,3,2:T(8,128)S(1)} %copy-done.4), kind=kOutput, calls=%fused_computation.1 | convolution fusion | flops 53747712 | bytes 1743552 | tf_op jit(solution)/shard_map/cxyk,jy->cxjk/dot_general | solution.py:138
  21.5 1.6 %convolution_bitcast_fusion.1 = f32[3,18,18,144]{3,1,2,0:T(8,128)S(1)} fusion(f32[18,24,1,1]{1,0,3,2:T(8,128)S(1)} %copy-done.4, f32[3,24,18,144]{3,2,1,0:T(8,128)S(1)} %convolution_bitcast_fusion), kind=kOutput, calls=%fused_computation.2 | convolution fusion | flops 40310784 | bytes 1308096 | tf_op jit(solution)/shard_map/cxjk,ix->cijk/dot_general | solution.py:144
  23.1 0.3 copy.30
  23.5 6.3 %reshape.6592 = f32[3,2,9,2,9,16,9]{6,5,4,3,2,1,0:T(8,128)} reshape(f32[3,18,18,144]{3,2,1,0:T(8,128)S(1)} %copy.30) | data formatting | bytes 1119744 | tf_op jit(solution)/shard_map/reshape | solution.py:161
  29.8 11.0 %copy.31 = f32[3,9,9,9,2,2,16]{6,5,4,0,3,2,1:T(2,128)} copy(f32[3,9,9,9,2,2,16]{3,6,2,5,1,4,0:T(8,128)} %bitcast.897) | data formatting | bytes 1119744 | tf_op jit(solution)/shard_map/transpose | solution.py:162
  40.8 5.8 %reshape.6593 = f32[3,9,9,9,64]{4,0,3,2,1:T(4,128)S(1)} reshape(f32[3,9,9,9,2,2,16]{6,5,4,0,3,2,1:T(2,128)} %copy.31) | data formatting | bytes 1119744 | tf_op jit(solution)/shard_map/reshape | solution.py:162
  46.7 0.8 fusion.125
  47.6 0.1 multiply_dynamic-update-slice_fusion.2
  47.7 0.0 copy-start.5
  47.7 0.1 multiply_dynamic-update-slice_fusion.1
  47.8 0.1 multiply_dynamic-update-slice_fusion
  47.9 0.6 copy-done.5
  48.5 2.9 %fusion.158 = f32[6,24,24,32]{3,2,1,0:T(8,128)S(1)} fusion(f32[6,24,24,136]{3,2,1,0:T(8,128)S(1)} %multiply_dynamic-update-slice_fusion, f32[32,136,1,1]{1,0,3,2:T(8,128)S(1)} %copy-done.5), kind=kOutput, calls=%fused_computation.409 | convolution fusion | flops 180486144 | bytes 2339840 | tf_op jit(solution)/shard_map/cxyz,kz->cxyk/dot_general | solution.py:132
  51.4 1.0 convolution_bitcast_fusion.2
  52.5 0.3 convolution_bitcast_fusion.3
  52.8 0.2 copy.28
  52.9 2.0 %slice_reduce_fusion = (f32[2,2,16]{2,1,0:T(2,128)S(1)}, f32[2,2,16]{2,1,0:T(2,128)S(1)}, f32[2,2,16]{2,1,0:T(2,128)S(1)}, f32[2,2,16]{2,1,0:T(2,128)S(1)}, f32[...) fusion(f32[6,2,2,2,2,16,2]{0,6,5,4,3,2,1:T(2,128)S(1)} %bitcast.898), kind=kLoop, calls=%fused_computation.34 | loop fusion | bytes 6144 | tf_op jit(solution)/shard_map/slice | solution.py:97
  55.0 0.1 squeeze.35
  55.1 0.1 squeeze.34
  55.1 0.1 squeeze.33
  55.2 0.1 squeeze.32
  55.3 0.1 squeeze.31
  55.4 0.1 squeeze.30
  55.5 0.1 squeeze.29
  55.6 0.1 squeeze.28
  55.6 0.1 squeeze.27
  55.7 0.1 squeeze.26
  55.8 0.1 squeeze.25
  55.9 0.1 squeeze.24
  56.4 0.3 stack.8
  56.7 0.3 concatenate.21
  57.0 0.2 fusion.159
  57.3 40.3 %psum.7 = f32[102,102]{1,0:T(8,128)S(1)} all-reduce(f32[102,102]{1,0:T(8,128)S(1)} %fusion.159), channel_id=1, replica_groups=mesh['gx'=4,'gy'=4,'gz'=2] {'gx','gy','gz'}, use_global_device_ids=true, to_apply=%region_0.0 | all-reduce | flops 10404 | bytes 83232 | tf_op jit(solution)/shard_map/psum | solution.py:174
  97.6 1.7 %gather_fusion = f32[102]{0:T(128)S(1)} fusion(f32[102,102]{1,0:T(8,128)S(1)} %psum.7, s32[102]{0:T(128)S(1)} %or_bitcast_fusion), kind=kCustom, calls=%fused_computation | custom fusion | bytes 1632 | tf_op jit(solution)/shard_map/jit(diagonal)/cond/branch_0_fun/gather | solution.py:108
  99.3 0.1 slice.404
  99.3 0.1 fusion.5
  99.4 0.1 copy.32
  99.5 0.1 fusion.8
  99.6 8.8 %cholesky.16 = f32[96,96]{1,0:T(8,128)S(1)} custom-call(f32[96,96]{1,0:T(8,128)S(1)} %fusion.8), custom_call_target="Cholesky" | custom-call | tf_op jit(solution)/shard_map/jit(cholesky)/cholesky | solution.py:114
  108.4 0.6 compare_reduce_fusion
  109.1 0.7 fusion.3
  109.7 7.4 %custom-call.10 = f32[1,96,96]{1,2,0:T(8,128)S(1)} custom-call(f32[1,96,96]{2,1,0:T(8,128)S(1)} %fusion.3), custom_call_target="InvertDiagBlocksLowerTriangular" | custom-call | tf_op jit(solution)/shard_map/jit(_cho_solve)/triangular_solve | solution.py:115
  117.1 0.3 fusion.4
  117.4 0.2 convolution_divide_fusion
  117.6 0.8 fusion.1
  (46 shorter events, 0.6 us)
Async XLA Ops:
  1.7 16.9 %copy-start.8 = (f32[144,136,1,1]{0,1,3,2:T(8,128)S(1)}, f32[144,136,1,1]{0,1,3,2:T(8,128)}, u32[]{:S(2)}) copy-start(f32[144,136,1,1]{0,1,3,2:T(8,128)} %constant.98) | copy-start | bytes 235012
  1.7 7.3 %collective-permute-start = (bf16[3,4,16,128]{3,2,1,0:T(8,128)(2,1)S(1)}, bf16[3,4,16,128]{3,2,1,0:T(8,128)(2,1)S(1)}, u32[]{:S(2)}, u32[]{:S(2)}) collective-permute-start(bf16[3,4,16,128]{3,2,1,0:T(8,128)(2,1)S(1)} %get-tuple-element.102), channel_id=1, source_target_pairs={{0,8},{8,16},{16,24},{24,0},{1,9},{9,17},{17,25},{25,1},{2,10},{10... | collective-permute-start | bytes 147464 | tf_op jit(solution)/shard_map/ppermute | solution.py:18
  4.8 4.6 %collective-permute-start.1 = (bf16[3,4,16,128]{3,2,1,0:T(8,128)(2,1)S(1)}, bf16[3,4,16,128]{3,2,1,0:T(8,128)(2,1)S(1)}, u32[]{:S(2)}, u32[]{:S(2)}) collective-permute-start(bf16[3,4,16,128]{3,2,1,0:T(8,128)(2,1)S(1)} %get-tuple-element.103), channel_id=1, source_target_pairs={{8,0},{16,8},{24,16},{0,24},{9,1},{17,9},{25,17},{1,25},{10,2},{18... | collective-permute-start | bytes 147464 | tf_op jit(solution)/shard_map/ppermute | solution.py:21
  9.4 10.5 %copy-start.2 = (bf16[3,4,16,128]{3,2,1,0:T(8,128)(2,1)}, bf16[3,4,16,128]{3,2,1,0:T(8,128)(2,1)S(1)}, u32[]{:S(2)}) copy-start(bf16[3,4,16,128]{3,2,1,0:T(8,128)(2,1)S(1)} %collective-permute-done.1) | copy-start | bytes 147460
  9.5 5.3 %collective-permute-start.2 = (bf16[3,24,4,128]{3,2,1,0:T(4,128)(2,1)S(1)}, bf16[3,24,4,128]{3,2,1,0:T(4,128)(2,1)S(1)}, u32[]{:S(2)}, u32[]{:S(2)}) collective-permute-start(bf16[3,24,4,128]{3,2,1,0:T(4,128)(2,1)S(1)} %get-tuple-element.100), channel_id=1, source_target_pairs={{0,2},{2,4},{4,6},{6,0},{1,3},{3,5},{5,7},{7,1},{8,10},{10,12},{12... | collective-permute-start | bytes 221192 | tf_op jit(solution)/shard_map/ppermute | solution.py:18
  11.0 4.6 %collective-permute-start.3 = (bf16[3,24,4,128]{3,2,1,0:T(4,128)(2,1)S(1)}, bf16[3,24,4,128]{3,2,1,0:T(4,128)(2,1)S(1)}, u32[]{:S(2)}, u32[]{:S(2)}) collective-permute-start(bf16[3,24,4,128]{3,2,1,0:T(4,128)(2,1)S(1)} %get-tuple-element.101), channel_id=1, source_target_pairs={{2,0},{4,2},{6,4},{0,6},{3,1},{5,3},{7,5},{1,7},{10,8},{12,10},{14... | collective-permute-start | bytes 221192 | tf_op jit(solution)/shard_map/ppermute | solution.py:21
  16.1 1.9 %collective-permute-start.4 = (bf16[3,24,24,4]{3,2,1,0:T(8,128)(2,1)S(1)}, bf16[3,24,24,4]{3,2,1,0:T(8,128)(2,1)S(1)}, u32[]{:S(2)}, u32[]{:S(2)}) collective-permute-start(bf16[3,24,24,4]{3,2,1,0:T(8,128)(2,1)S(1)} %get-tuple-element.98), channel_id=1, source_target_pairs={{0,1},{1,0},{2,3},{3,2},{4,5},{5,4},{6,7},{7,6},{8,9},{9,8},{10,11... | collective-permute-start | bytes 41480 | tf_op jit(solution)/shard_map/ppermute | solution.py:18
  16.2 2.4 %collective-permute-start.5 = (bf16[3,24,24,4]{3,2,1,0:T(8,128)(2,1)S(1)}, bf16[3,24,24,4]{3,2,1,0:T(8,128)(2,1)S(1)}, u32[]{:S(2)}, u32[]{:S(2)}) collective-permute-start(bf16[3,24,24,4]{3,2,1,0:T(8,128)(2,1)S(1)} %get-tuple-element.99), channel_id=1, source_target_pairs={{1,0},{0,1},{3,2},{2,3},{5,4},{4,5},{7,6},{6,7},{9,8},{8,9},{11,10... | collective-permute-start | bytes 41480 | tf_op jit(solution)/shard_map/ppermute | solution.py:21
  16.7 3.3 %copy-start.4 = (f32[18,24,1,1]{1,0,3,2:T(8,128)S(1)}, f32[18,24,1,1]{1,0,3,2:T(8,128)}, u32[]{:S(2)}) copy-start(f32[18,24,1,1]{1,0,3,2:T(8,128)} %constant.99) | copy-start | bytes 5188
  18.6 1.3 %copy-start = (bf16[3,24,24,4]{3,2,1,0:T(8,128)(2,1)}, bf16[3,24,24,4]{3,2,1,0:T(8,128)(2,1)S(1)}, u32[]{:S(2)}) copy-start(bf16[3,24,24,4]{3,2,1,0:T(8,128)(2,1)S(1)} %collective-permute-done.5) | copy-start | bytes 41476
  40.8 5.9 %copy-start.1 = (bf16[3,24,24,4]{3,2,1,0:T(8,128)(2,1)S(1)}, bf16[3,24,24,4]{3,2,1,0:T(8,128)(2,1)}, u32[]{:S(2)}) copy-start(bf16[3,24,24,4]{3,2,1,0:T(8,128)(2,1)} %copy-done) | copy-start | bytes 41476
  40.8 5.9 %copy-start.3 = (bf16[3,4,16,128]{3,2,1,0:T(8,128)(2,1)S(1)}, bf16[3,4,16,128]{3,2,1,0:T(8,128)(2,1)}, u32[]{:S(2)}) copy-start(bf16[3,4,16,128]{3,2,1,0:T(8,128)(2,1)} %copy-done.2) | copy-start | bytes 147460
  47.7 0.8 copy-start.5
  48.5 2.9 %copy-start.6 = (f32[4,24,1,1]{1,0,3,2:T(4,128)S(1)}, f32[4,24,1,1]{1,0,3,2:T(4,128)}, u32[]{:S(2)}) copy-start(f32[4,24,1,1]{1,0,3,2:T(4,128)} %constant.97) | copy-start | bytes 1156
  117.6 0.8 copy-start.7
where the time goes:
time: 119 us; the launch traced here: 118 us
  blocking collectives  40.3 us (34%)
  local copies, waits for them, and re-layouts  29.8 us (25%)
  other arithmetic  20.6 us (17%)
  matrix products  10.3 us (9%)
  starting transfers between devices  8.74 us (7%)
  waiting for transfers between devices  7.6 us (6%)
    psum x1, blocking collectives, shards(): gram_matrix = lax.psum(local_gram, ('gx', 'gy', 'gz'))  40.3 us
    transpose x1, local copies, waits for them, and re-layouts, shards(): jnp.transpose(box_means, (0, 2, 4, 6, 1, 3, 5)).reshape(3, 9, 9, 9, samples)  11 us
    another operation x3, other arithmetic, solve_fit(): factor = jnp.linalg.cholesky(normal)  9.45 us
    another operation x2, other arithmetic, solve_fit(): solved = jax.scipy.linalg.cho_solve((factor, True), target_side)  8.01 us
    reshape x1, local copies, waits for them, and re-layouts, shards(): box_means = box_means.reshape(3, count_x, 9, count_y, 9, count_z, 9)  6.35 us
    reshape x1, local copies, waits for them, and re-layouts, shards(): jnp.transpose(box_means, (0, 2, 4, 6, 1, 3, 5)).reshape(3, 9, 9, 9, samples)  5.76 us
    ppermute x3, waiting for transfers between devices, extended(): lax.ppermute(lax.slice_in_dim(block, block.shape[dim] - width, None, axis...  5.7 us
    ppermute x3, starting transfers between devices, extended(): lax.ppermute(lax.slice_in_dim(block, block.shape[dim] - width, None, axis...  4.72 us
  transfers between devices with their start and end apart: 6, of which 6 were waited for; matrix products, arithmetic and copies ran while one was open for 0% of the time, Pallas kernels for 0%

commit v1 on v0

--- a/solution.py
+++ b/solution.py
@@ -7,6 +7,7 @@
 PRECISE = lax.Precision.HIGHEST
 INDEX_PAIRS = ((0, 0), (1, 1), (2, 2), (0, 1), (0, 2), (1, 2))
 WIDTHS = (3.0, 6.0, 12.0)
+bars_handle = lambda inputs: lax.psum(lax.psum(inputs, ("gy", "gz")), "gx")
 
 
 def extended(block, sides, width):
@@ -171,7 +172,7 @@
     features, targets = build_rows(box_means, pair_means)
     stacked = jnp.concatenate([features, targets], axis=0)
     local_gram = jnp.dot(stacked, stacked.T, precision=PRECISE, preferred_element_type=jnp.float32)
-    gram_matrix = lax.psum(local_gram, ("gx", "gy", "gz"))
+    gram_matrix = bars_handle(local_gram)
     sample_total = float(samples * lax.axis_size("gx") * lax.axis_size("gy") * lax.axis_size("gz"))
     coefficients, target_scale = solve_fit(gram_matrix, sample_total)
     predicted = jnp.dot(

time: 119 us -> 123 us (1.034)
  blocking collectives: 40.3 us -> 44.1 us
    psum x1 -> x2, blocking collectives: 40.3 us -> 44.1 us  [bars_handle = lambda inputs: lax.psum(lax.psum(inputs, ('gy', 'gz')), 'gx')]
where the time goes in v1:
time: 123 us; the launch traced here: 122 us
  blocking collectives  44.1 us (36%)
  local copies, waits for them, and re-layouts  29.8 us (24%)
  other arithmetic  20.6 us (17%)
  matrix products  10.3 us (8%)
  starting transfers between devices  8.74 us (7%)
  waiting for transfers between devices  7.6 us (6%)
    psum x2, blocking collectives, bars_handle = lambda inputs: lax.psum(lax.psum(inputs, ('gy', 'gz')), 'gx')  44.1 us
    transpose x1, local copies, waits for them, and re-layouts, shards(): jnp.transpose(box_means, (0, 2, 4, 6, 1, 3, 5)).reshape(3, 9, 9, 9, samples)  11 us
    another operation x3, other arithmetic, solve_fit(): factor = jnp.linalg.cholesky(normal)  9.45 us
    another operation x2, other arithmetic, solve_fit(): solved = jax.scipy.linalg.cho_solve((factor, True), target_side)  8.01 us
    reshape x1, local copies, waits for them, and re-layouts, shards(): box_means = box_means.reshape(3, count_x, 9, count_y, 9, count_z, 9)  6.35 us
    reshape x1, local copies, waits for them, and re-layouts, shards(): jnp.transpose(box_means, (0, 2, 4, 6, 1, 3, 5)).reshape(3, 9, 9, 9, samples)  5.76 us
    ppermute x3, waiting for transfers between devices, extended(): lax.ppermute(lax.slice_in_dim(block, block.shape[dim] - width, None, axis...  5.7 us
    ppermute x3, starting transfers between devices, extended(): lax.ppermute(lax.slice_in_dim(block, block.shape[dim] - width, None, axis...  4.72 us
  transfers between devices with their start and end apart: 6, of which 6 were waited for; matrix products, arithmetic and copies ran while one was open for 0% of the time, Pallas kernels for 0%

profile of v1, /device:TPU:0, one launch (start us, length us, event | category | flops | bytes accessed | tf_op | source)
XLA Modules:
  0.0 122.2 jit_solution(15691184890532090186)
XLA Ops:
  0.6 1.0 convert_element_type.7
  1.7 0.0 copy-start.8
  1.7 3.1 %collective-permute-start = (bf16[3,4,16,128]{3,2,1,0:T(8,128)(2,1)S(1)}, bf16[3,4,16,128]{3,2,1,0:T(8,128)(2,1)S(1)}, u32[]{:S(2)}, u32[]{:S(2)}) collective-permute-start(bf16[3,4,16,128]{3,2,1,0:T(8,128)(2,1)S(1)} %get-tuple-element.102), channel_id=1, source_target_pairs={{0,8},{8,16},{16,24},{24,0},{1,9},{9,17},{17,25},{25,1},{2,10},{10... | collective-permute-start | bytes 147464 | tf_op jit(solution)/shard_map/ppermute | solution.py:19
  4.8 2.1 %collective-permute-start.1 = (bf16[3,4,16,128]{3,2,1,0:T(8,128)(2,1)S(1)}, bf16[3,4,16,128]{3,2,1,0:T(8,128)(2,1)S(1)}, u32[]{:S(2)}, u32[]{:S(2)}) collective-permute-start(bf16[3,4,16,128]{3,2,1,0:T(8,128)(2,1)S(1)} %get-tuple-element.103), channel_id=1, source_target_pairs={{8,0},{16,8},{24,16},{0,24},{9,1},{17,9},{25,17},{1,25},{10,2},{18... | collective-permute-start | bytes 147464 | tf_op jit(solution)/shard_map/ppermute | solution.py:22
  6.9 2.1 %collective-permute-done = bf16[3,4,16,128]{3,2,1,0:T(8,128)(2,1)S(1)} collective-permute-done((bf16[3,4,16,128]{3,2,1,0:T(8,128)(2,1)S(1)}, bf16[3,4,16,128]{3,2,1,0:T(8,128)(2,1)S(1)}, u32[]{:S(2)}, u32[]{:S(2)}) %collective-permute-start) | collective-permute-done | bytes 49184 | tf_op jit(solution)/shard_map/ppermute | solution.py:19
  9.0 0.4 collective-permute-done.1
  9.4 0.1 pad_maximum_fusion.4
  9.5 1.5 %collective-permute-start.2 = (bf16[3,24,4,128]{3,2,1,0:T(4,128)(2,1)S(1)}, bf16[3,24,4,128]{3,2,1,0:T(4,128)(2,1)S(1)}, u32[]{:S(2)}, u32[]{:S(2)}) collective-permute-start(bf16[3,24,4,128]{3,2,1,0:T(4,128)(2,1)S(1)} %get-tuple-element.100), channel_id=1, source_target_pairs={{0,2},{2,4},{4,6},{6,0},{1,3},{3,5},{5,7},{7,1},{8,10},{10,12},{12... | collective-permute-start | bytes 221192 | tf_op jit(solution)/shard_map/ppermute | solution.py:19
  11.0 1.4 %collective-permute-start.3 = (bf16[3,24,4,128]{3,2,1,0:T(4,128)(2,1)S(1)}, bf16[3,24,4,128]{3,2,1,0:T(4,128)(2,1)S(1)}, u32[]{:S(2)}, u32[]{:S(2)}) collective-permute-start(bf16[3,24,4,128]{3,2,1,0:T(4,128)(2,1)S(1)} %get-tuple-element.101), channel_id=1, source_target_pairs={{2,0},{4,2},{6,4},{0,6},{3,1},{5,3},{7,5},{1,7},{10,8},{12,10},{14... | collective-permute-start | bytes 221192 | tf_op jit(solution)/shard_map/ppermute | solution.py:22
  12.5 2.3 %collective-permute-done.2 = bf16[3,24,4,128]{3,2,1,0:T(4,128)(2,1)S(1)} collective-permute-done((bf16[3,24,4,128]{3,2,1,0:T(4,128)(2,1)S(1)}, bf16[3,24,4,128]{3,2,1,0:T(4,128)(2,1)S(1)}, u32[]{:S(2)}, u32[]{:S(2)}) %collective-permute-start.2) | collective-permute-done | bytes 73760 | tf_op jit(solution)/shard_map/ppermute | solution.py:19
  14.8 0.8 collective-permute-done.3
  15.6 0.2 pad_maximum_fusion.1
  15.9 0.2 fusion.156
  16.1 0.1 collective-permute-start.4
  16.2 0.5 collective-permute-start.5
  16.7 1.3 %collective-permute-done.4 = bf16[3,24,24,4]{3,2,1,0:T(8,128)(2,1)S(1)} collective-permute-done((bf16[3,24,24,4]{3,2,1,0:T(8,128)(2,1)S(1)}, bf16[3,24,24,4]{3,2,1,0:T(8,128)(2,1)S(1)}, u32[]{:S(2)}, u32[]{:S(2)}) %collective-permute-start.4) | collective-permute-done | bytes 13856 | tf_op jit(solution)/shard_map/ppermute | solution.py:19
  17.9 0.6 collective-permute-done.5
  18.6 1.3 %fusion.124 = f32[3,24,24,144]{3,2,1,0:T(8,128)S(1)} fusion(f32[144,136,1,1]{0,1,3,2:T(8,128)S(1)} %copy-done.8, bf16[3,24,24,4]{3,2,1,0:T(8,128)(2,1)S(1)} %collective-permute-done.5, bf16[3,24,4,128]{3,2,1,0:T(4,128)(2,1)S(1)} %collective-permute-done.3, bf16[3,4,16,128]{3,2,1,0:T(8,128)(2,1)S(1)} %collective-permute-done.1, ...), kind=kOutput, calls=%fused_computation.402 | convolution fusion | flops 409383936 | bytes 1543680 | tf_op jit(solution)/shard_map/cxyz,kz->cxyk/dot_general | solution.py:133
  19.9 1.6 %convolution_bitcast_fusion = f32[3,24,18,144]{3,2,1,0:T(8,128)S(1)} fusion(f32[3,24,24,144]{3,2,1,0:T(8,128)S(1)} %fusion.124, f32[18,24,1,1]{1,0,3,2:T(8,128)S(1)} %copy-done.4), kind=kOutput, calls=%fused_computation.1 | convolution fusion | flops 53747712 | bytes 1743552 | tf_op jit(solution)/shard_map/cxyk,jy->cxjk/dot_general | solution.py:139
  21.5 1.6 %convolution_bitcast_fusion.1 = f32[3,18,18,144]{3,1,2,0:T(8,128)S(1)} fusion(f32[18,24,1,1]{1,0,3,2:T(8,128)S(1)} %copy-done.4, f32[3,24,18,144]{3,2,1,0:T(8,128)S(1)} %convolution_bitcast_fusion), kind=kOutput, calls=%fused_computation.2 | convolution fusion | flops 40310784 | bytes 1308096 | tf_op jit(solution)/shard_map/cxjk,ix->cijk/dot_general | solution.py:145
  23.1 0.3 copy.30
  23.5 6.3 %reshape.6592 = f32[3,2,9,2,9,16,9]{6,5,4,3,2,1,0:T(8,128)} reshape(f32[3,18,18,144]{3,2,1,0:T(8,128)S(1)} %copy.30) | data formatting | bytes 1119744 | tf_op jit(solution)/shard_map/reshape | solution.py:162
  29.8 11.0 %copy.31 = f32[3,9,9,9,2,2,16]{6,5,4,0,3,2,1:T(2,128)} copy(f32[3,9,9,9,2,2,16]{3,6,2,5,1,4,0:T(8,128)} %bitcast.897) | data formatting | bytes 1119744 | tf_op jit(solution)/shard_map/transpose | solution.py:163
  40.8 5.8 %reshape.6593 = f32[3,9,9,9,64]{4,0,3,2,1:T(4,128)S(1)} reshape(f32[3,9,9,9,2,2,16]{6,5,4,0,3,2,1:T(2,128)} %copy.31) | data formatting | bytes 1119744 | tf_op jit(solution)/shard_map/reshape | solution.py:163
  46.7 0.8 fusion.125
  47.6 0.1 multiply_dynamic-update-slice_fusion.2
  47.7 0.0 copy-start.5
  47.7 0.1 multiply_dynamic-update-slice_fusion.1
  47.8 0.1 multiply_dynamic-update-slice_fusion
  47.9 0.6 copy-done.5
  48.5 2.9 %fusion.158 = f32[6,24,24,32]{3,2,1,0:T(8,128)S(1)} fusion(f32[6,24,24,136]{3,2,1,0:T(8,128)S(1)} %multiply_dynamic-update-slice_fusion, f32[32,136,1,1]{1,0,3,2:T(8,128)S(1)} %copy-done.5), kind=kOutput, calls=%fused_computation.409 | convolution fusion | flops 180486144 | bytes 2339840 | tf_op jit(solution)/shard_map/cxyz,kz->cxyk/dot_general | solution.py:133
  51.4 1.0 convolution_bitcast_fusion.2
  52.5 0.3 convolution_bitcast_fusion.3
  52.8 0.2 copy.28
  52.9 2.0 %slice_reduce_fusion = (f32[2,2,16]{2,1,0:T(2,128)S(1)}, f32[2,2,16]{2,1,0:T(2,128)S(1)}, f32[2,2,16]{2,1,0:T(2,128)S(1)}, f32[2,2,16]{2,1,0:T(2,128)S(1)}, f32[...) fusion(f32[6,2,2,2,2,16,2]{0,6,5,4,3,2,1:T(2,128)S(1)} %bitcast.898), kind=kLoop, calls=%fused_computation.34 | loop fusion | bytes 6144 | tf_op jit(solution)/shard_map/slice | solution.py:98
  55.0 0.1 squeeze.35
  55.1 0.1 squeeze.34
  55.1 0.1 squeeze.33
  55.2 0.1 squeeze.32
  55.3 0.1 squeeze.31
  55.4 0.1 squeeze.30
  55.5 0.1 squeeze.29
  55.6 0.1 squeeze.28
  55.6 0.1 squeeze.27
  55.7 0.1 squeeze.26
  55.8 0.1 squeeze.25
  55.9 0.1 squeeze.24
  56.4 0.3 stack.8
  56.7 0.3 concatenate.21
  57.0 0.2 fusion.159
  57.3 24.5 %psum.14 = f32[102,102]{1,0:T(8,128)S(1)} all-reduce(f32[102,102]{1,0:T(8,128)S(1)} %fusion.159), channel_id=1, replica_groups=mesh['gx'=4,'gy'=4,'gz'=2] {'gy','gz'}, use_global_device_ids=true, to_apply=%region_0.0 | all-reduce | flops 10404 | bytes 83232 | tf_op jit(solution)/shard_map/psum | solution.py:10
  81.7 19.6 %psum.15 = f32[102,102]{1,0:T(8,128)S(1)} all-reduce(f32[102,102]{1,0:T(8,128)S(1)} %psum.14), channel_id=1, replica_groups=mesh['gx'=4,'gy'=4,'gz'=2] {'gx'}, use_global_device_ids=true, to_apply=%region_1.0 | all-reduce | flops 10404 | bytes 83232 | tf_op jit(solution)/shard_map/psum | solution.py:10
  101.4 1.7 %gather_fusion = f32[102]{0:T(128)S(1)} fusion(f32[102,102]{1,0:T(8,128)S(1)} %psum.15, s32[102]{0:T(128)S(1)} %or_bitcast_fusion), kind=kCustom, calls=%fused_computation | custom fusion | bytes 1632 | tf_op jit(solution)/shard_map/jit(diagonal)/cond/branch_0_fun/gather | solution.py:109
  103.1 0.1 slice.404
  103.2 0.1 fusion.5
  103.3 0.1 copy.32
  103.4 0.1 fusion.8
  103.5 8.8 %cholesky.16 = f32[96,96]{1,0:T(8,128)S(1)} custom-call(f32[96,96]{1,0:T(8,128)S(1)} %fusion.8), custom_call_target="Cholesky" | custom-call | tf_op jit(solution)/shard_map/jit(cholesky)/cholesky | solution.py:115
  112.3 0.6 compare_reduce_fusion
  112.9 0.7 fusion.3
  113.6 7.4 %custom-call.10 = f32[1,96,96]{1,2,0:T(8,128)S(1)} custom-call(f32[1,96,96]{2,1,0:T(8,128)S(1)} %fusion.3), custom_call_target="InvertDiagBlocksLowerTriangular" | custom-call | tf_op jit(solution)/shard_map/jit(_cho_solve)/triangular_solve | solution.py:116
  120.9 0.3 fusion.4
  121.2 0.2 convolution_divide_fusion
  121.4 0.8 fusion.1
  (47 shorter events, 0.6 us)
Async XLA Ops:
  1.7 16.9 %copy-start.8 = (f32[144,136,1,1]{0,1,3,2:T(8,128)S(1)}, f32[144,136,1,1]{0,1,3,2:T(8,128)}, u32[]{:S(2)}) copy-start(f32[144,136,1,1]{0,1,3,2:T(8,128)} %constant.98) | copy-start | bytes 235012
  1.7 7.3 %collective-permute-start = (bf16[3,4,16,128]{3,2,1,0:T(8,128)(2,1)S(1)}, bf16[3,4,16,128]{3,2,1,0:T(8,128)(2,1)S(1)}, u32[]{:S(2)}, u32[]{:S(2)}) collective-permute-start(bf16[3,4,16,128]{3,2,1,0:T(8,128)(2,1)S(1)} %get-tuple-element.102), channel_id=1, source_target_pairs={{0,8},{8,16},{16,24},{24,0},{1,9},{9,17},{17,25},{25,1},{2,10},{10... | collective-permute-start | bytes 147464 | tf_op jit(solution)/shard_map/ppermute | solution.py:19
  4.8 4.6 %collective-permute-start.1 = (bf16[3,4,16,128]{3,2,1,0:T(8,128)(2,1)S(1)}, bf16[3,4,16,128]{3,2,1,0:T(8,128)(2,1)S(1)}, u32[]{:S(2)}, u32[]{:S(2)}) collective-permute-start(bf16[3,4,16,128]{3,2,1,0:T(8,128)(2,1)S(1)} %get-tuple-element.103), channel_id=1, source_target_pairs={{8,0},{16,8},{24,16},{0,24},{9,1},{17,9},{25,17},{1,25},{10,2},{18... | collective-permute-start | bytes 147464 | tf_op jit(solution)/shard_map/ppermute | solution.py:22
  9.4 10.5 %copy-start.2 = (bf16[3,4,16,128]{3,2,1,0:T(8,128)(2,1)}, bf16[3,4,16,128]{3,2,1,0:T(8,128)(2,1)S(1)}, u32[]{:S(2)}) copy-start(bf16[3,4,16,128]{3,2,1,0:T(8,128)(2,1)S(1)} %collective-permute-done.1) | copy-start | bytes 147460
  9.5 5.3 %collective-permute-start.2 = (bf16[3,24,4,128]{3,2,1,0:T(4,128)(2,1)S(1)}, bf16[3,24,4,128]{3,2,1,0:T(4,128)(2,1)S(1)}, u32[]{:S(2)}, u32[]{:S(2)}) collective-permute-start(bf16[3,24,4,128]{3,2,1,0:T(4,128)(2,1)S(1)} %get-tuple-element.100), channel_id=1, source_target_pairs={{0,2},{2,4},{4,6},{6,0},{1,3},{3,5},{5,7},{7,1},{8,10},{10,12},{12... | collective-permute-start | bytes 221192 | tf_op jit(solution)/shard_map/ppermute | solution.py:19
  11.0 4.6 %collective-permute-start.3 = (bf16[3,24,4,128]{3,2,1,0:T(4,128)(2,1)S(1)}, bf16[3,24,4,128]{3,2,1,0:T(4,128)(2,1)S(1)}, u32[]{:S(2)}, u32[]{:S(2)}) collective-permute-start(bf16[3,24,4,128]{3,2,1,0:T(4,128)(2,1)S(1)} %get-tuple-element.101), channel_id=1, source_target_pairs={{2,0},{4,2},{6,4},{0,6},{3,1},{5,3},{7,5},{1,7},{10,8},{12,10},{14... | collective-permute-start | bytes 221192 | tf_op jit(solution)/shard_map/ppermute | solution.py:22
  16.1 1.9 %collective-permute-start.4 = (bf16[3,24,24,4]{3,2,1,0:T(8,128)(2,1)S(1)}, bf16[3,24,24,4]{3,2,1,0:T(8,128)(2,1)S(1)}, u32[]{:S(2)}, u32[]{:S(2)}) collective-permute-start(bf16[3,24,24,4]{3,2,1,0:T(8,128)(2,1)S(1)} %get-tuple-element.98), channel_id=1, source_target_pairs={{0,1},{1,0},{2,3},{3,2},{4,5},{5,4},{6,7},{7,6},{8,9},{9,8},{10,11... | collective-permute-start | bytes 41480 | tf_op jit(solution)/shard_map/ppermute | solution.py:19
  16.2 2.4 %collective-permute-start.5 = (bf16[3,24,24,4]{3,2,1,0:T(8,128)(2,1)S(1)}, bf16[3,24,24,4]{3,2,1,0:T(8,128)(2,1)S(1)}, u32[]{:S(2)}, u32[]{:S(2)}) collective-permute-start(bf16[3,24,24,4]{3,2,1,0:T(8,128)(2,1)S(1)} %get-tuple-element.99), channel_id=1, source_target_pairs={{1,0},{0,1},{3,2},{2,3},{5,4},{4,5},{7,6},{6,7},{9,8},{8,9},{11,10... | collective-permute-start | bytes 41480 | tf_op jit(solution)/shard_map/ppermute | solution.py:22
  16.7 3.3 %copy-start.4 = (f32[18,24,1,1]{1,0,3,2:T(8,128)S(1)}, f32[18,24,1,1]{1,0,3,2:T(8,128)}, u32[]{:S(2)}) copy-start(f32[18,24,1,1]{1,0,3,2:T(8,128)} %constant.99) | copy-start | bytes 5188
  18.6 1.3 %copy-start = (bf16[3,24,24,4]{3,2,1,0:T(8,128)(2,1)}, bf16[3,24,24,4]{3,2,1,0:T(8,128)(2,1)S(1)}, u32[]{:S(2)}) copy-start(bf16[3,24,24,4]{3,2,1,0:T(8,128)(2,1)S(1)} %collective-permute-done.5) | copy-start | bytes 41476
  40.8 5.9 %copy-start.1 = (bf16[3,24,24,4]{3,2,1,0:T(8,128)(2,1)S(1)}, bf16[3,24,24,4]{3,2,1,0:T(8,128)(2,1)}, u32[]{:S(2)}) copy-start(bf16[3,24,24,4]{3,2,1,0:T(8,128)(2,1)} %copy-done) | copy-start | bytes 41476
  40.8 5.9 %copy-start.3 = (bf16[3,4,16,128]{3,2,1,0:T(8,128)(2,1)S(1)}, bf16[3,4,16,128]{3,2,1,0:T(8,128)(2,1)}, u32[]{:S(2)}) copy-start(bf16[3,4,16,128]{3,2,1,0:T(8,128)(2,1)} %copy-done.2) | copy-start | bytes 147460
  47.7 0.8 copy-start.5
  48.5 2.9 %copy-start.6 = (f32[4,24,1,1]{1,0,3,2:T(4,128)S(1)}, f32[4,24,1,1]{1,0,3,2:T(4,128)}, u32[]{:S(2)}) copy-start(f32[4,24,1,1]{1,0,3,2:T(4,128)} %constant.97) | copy-start | bytes 1156
  121.4 0.8 copy-start.7
